TPU v7x, 32 devices: a whole 2x2x4 slice. The times are simulated.
32 devices in a mesh: vec: 16 (over z, y, x), row: 2 (over core).
Axes of the slice: x: 2, y: 2, z: 4, core: 2. Of those that a mesh axis runs over, the one named last changes fastest.
Arguments:
- vectors: bfloat16 [2, 4096, 1024], P('row', 'vec'), may hold values from -6 to 6
- rotation: bfloat16 [1024, 1024], P(None, 'vec'), may hold values from -0.1875 to 0.1875
- blocks: bfloat16 [64, 8, 128, 128], P('row'), may hold values from -0.125 to 0.125
- column_blocks: int32 [64, 8], P('row'), may hold values from -2 to 65, as said below
Outputs:
- filtered: bfloat16 [2, 4096, 1024], P('row', 'vec')
Inputs may be any that keep to these rules, and one draw needn't show every extreme that they name: `column_blocks`: block row r of partition p = r // 32 lists 8 distinct column blocks between p * 32 - 2 and p * 32 + 33; the first block row of every partition lists the lowest of these and the last one the highest; column blocks outside 0 to 63 stand for zeros.
All inputs are finite; a program needn't handle non-finite values.
Results may differ from a plain program's by a relative error of at most 0.006.
Values may be sent and summed in bfloat16 or wider, within the bound.
No kernel may reach another device: no remote copies, remote signals or barrier semaphores. Data moves between devices by JAX's collectives and lax.ppermute only.
A program may use at most 64 MiB of HBM per device.

v0:
```python
import jax
import jax.numpy as jnp
from jax import lax
from jax.sharding import PartitionSpec as P

BS = 128
HB = 2
STEPS = 4
centre = 0.3
half_width = 1.2


def with_halo(block, sides, width):
    for axis, dim in sides:
        count = lax.axis_size(axis)
        forward = [(i, i + 1) for i in range(count - 1)]
        backward = [(target, source) for source, target in forward]
        low = lax.ppermute(
            lax.slice_in_dim(block, block.shape[dim] - width, None, axis=dim), axis, forward
        )
        high = lax.ppermute(lax.slice_in_dim(block, 0, width, axis=dim), axis, backward)
        block = jnp.concatenate([low, block, high], axis=dim)
    return block


def apply_matrix(operand, blocks, offsets):
    extended = with_halo(operand, (("row", 1),), HB * BS)
    stacked = extended.reshape(extended.shape[0], -1, BS)
    picked = stacked[:, offsets]
    product = jnp.einsum("rjab,krjb->kra", blocks, picked, preferred_element_type=jnp.float32)
    return product.reshape(extended.shape[0], -1)


def filter_panel(vec_panel, blocks, offsets):
    previous = vec_panel.astype(jnp.float32)
    current = (apply_matrix(vec_panel, blocks, offsets) - centre * previous) / half_width
    for turn_index in range(STEPS - 1):
        operand = current.astype(jnp.bfloat16)
        following = (
            2.0 * (apply_matrix(operand, blocks, offsets) - centre * current) / half_width
            - previous
        )
        previous = current
        current = following
    return current.astype(jnp.bfloat16)


def local(vectors, rotation, blocks, column_blocks):
    local_rows = vectors[0]
    offsets = column_blocks - (lax.axis_index("row") * column_blocks.shape[0] - HB)
    contract = (((0,), (1,)), ((), ()))
    rotated = lax.dot_general(
        lax.all_gather(rotation, "vec", axis=1, tiled=True),
        local_rows,
        contract,
        preferred_element_type=jnp.float32,
    ).astype(jnp.bfloat16)
    vec_panel = lax.all_to_all(rotated, "vec", split_axis=0, concat_axis=1, tiled=True)
    filtered = filter_panel(vec_panel, blocks, offsets)
    returned = lax.all_to_all(filtered, "vec", split_axis=1, concat_axis=0, tiled=True)
    return jnp.transpose(returned)[None]


def solution(mesh):
    placed = (P("row", "vec", None), P(None, "vec"), P("row", None, None, None), P("row", None))
    return jax.shard_map(
        local, mesh=mesh, in_specs=placed, out_specs=P("row", "vec", None), check_vma=False
    )
```

profile of v0, /device:TPU:0, one launch (start us, length us, event | category | flops | bytes accessed | tf_op | source)
XLA Modules:
  0.0 203.2 jit_solution(18180730329563429137)
XLA Ops:
  6.5 0.7 all-gather.2.cloned.1.call-update
  7.3 66.0 %all-gather.2.cloned.1.call-done = bf16[1024,1024]{0,1:T(8,128)(2,1)} async-done(((bf16[1024,64]{0,1:T(8,128)(2,1)}), bf16[1024,1024]{0,1:T(8,128)(2,1)}) %all-gather.2.cloned.1.call-update) | async-done | bytes 2097168 | tf_op jit(solution)/shard_map/all_gather | solution.py:53
  73.2 3.1 %convolution_convert_fusion = bf16[1024,256]{1,0:T(8,128)(2,1)} fusion(bf16[1024,1024]{0,1:T(8,128)(2,1)} %all-gather.2.cloned.1.call-done, bf16[1,256,1024]{2,1,0:T(8,128)(2,1)S(1)} %copy-done), kind=kOutput, calls=%fused_computation.9 | convolution fusion | flops 537133056 | bytes 3145728 | tf_op jit(solution)/shard_map/dot_general | solution.py:52
  76.4 4.4 %all-to-all-start = ((bf16[16,64,256]{2,1,0:T(8,128)(2,1)}), bf16[16,64,256]{2,1,0:T(8,128)(2,1)S(1)}, u32[]{:S(2)}, u32[]{:S(2)}) async-start(bf16[16,64,256]{2,1,0:T(8,128)(2,1)} %bitcast.1), calls=%async_computation | async-start | bytes 1048576 | tf_op jit(solution)/shard_map/all_to_all | solution.py:58
  80.8 0.1 copy.22
  80.9 0.1 reshape.53
  81.0 14.0 %all-to-all-done = bf16[16,64,256]{2,1,0:T(8,128)(2,1)S(1)} async-done(((bf16[16,64,256]{2,1,0:T(8,128)(2,1)}), bf16[16,64,256]{2,1,0:T(8,128)(2,1)S(1)}, u32[]{:S(2)}, u32[]{:S(2)}) %all-to-all-start) | async-done | bytes 524320 | tf_op jit(solution)/shard_map/all_to_all | solution.py:58
  95.0 0.0 copy-start.1
  95.0 1.3 collective-permute-start
  96.3 1.3 collective-permute-start.1
  97.7 0.0 collective-permute-done
  97.7 1.8 collective-permute-done.1
  99.4 0.2 copy_bitcast_fusion.3
  99.6 3.0 %gather_fusion = bf16[256,64,128]{2,1,0:T(8,128)(2,1)} fusion(bf16[64,36,128]{2,0,1:T(8,128)(2,1)S(1)} %copy_bitcast_fusion.3, s32[1024]{0:T(1024)S(1)} %pad_clamp_fusion), kind=kCustom, calls=%fused_computation | custom fusion | bytes 8389632 | tf_op jit(solution)/shard_map/gather | solution.py:29
  102.7 7.6 %fusion.12 = f32[32,64,128,1]{2,1,3,0:T(8,128)S(1)} fusion(bf16[64,32,8,128]{3,0,2,1:T(8,128)(2,1)} %bitcast.117, bf16[32,8,128,128]{3,2,1,0:T(8,128)(2,1)} %param.6), kind=kOutput, calls=%fused_computation.36 | convolution fusion | flops 536870912 | bytes 13631488 | tf_op jit(solution)/shard_map/rjab,krjb->kra/dot_general | solution.py:30
  110.3 0.2 multiply_convert_fusion
  110.5 2.1 %collective-permute-start.2 = (bf16[64,256]{1,0:T(8,128)(2,1)S(1)}, bf16[64,256]{1,0:T(8,128)(2,1)S(1)}, u32[]{:S(2)}, u32[]{:S(2)}) collective-permute-start(bf16[64,256]{1,0:T(8,128)(2,1)S(1)} %get-tuple-element.9), channel_id=1, source_target_pairs={{0,1},{2,3},{4,5},{6,7},{8,9},{10,11},{12,13},{14,15},{16,17},{18,... | collective-permute-start | bytes 98312 | tf_op jit(solution)/shard_map/ppermute | solution.py:18
  112.5 1.3 collective-permute-start.3
  113.8 1.8 collective-permute-done.3
  115.6 0.2 copy_bitcast_fusion.2
  115.8 3.0 %gather_fusion.1 = bf16[256,64,128]{2,1,0:T(8,128)(2,1)} fusion(bf16[64,36,128]{2,0,1:T(8,128)(2,1)S(1)} %copy_bitcast_fusion.2, s32[1024]{0:T(1024)S(1)} %pad_clamp_fusion), kind=kCustom, calls=%fused_computation.1 | custom fusion | bytes 8389632 | tf_op jit(solution)/shard_map/gather | solution.py:29
  118.8 7.6 %fusion.13 = f32[32,64,128,1]{2,1,3,0:T(8,128)S(1)} fusion(bf16[64,32,8,128]{3,0,2,1:T(8,128)(2,1)} %bitcast.118, bf16[32,8,128,128]{3,2,1,0:T(8,128)(2,1)} %param.6), kind=kOutput, calls=%fused_computation.37 | convolution fusion | flops 536870912 | bytes 13631488 | tf_op jit(solution)/shard_map/rjab,krjb->kra/dot_general | solution.py:30
  126.5 0.3 fusion.7
  126.8 2.1 %collective-permute-start.4 = (bf16[64,256]{1,0:T(8,128)(2,1)S(1)}, bf16[64,256]{1,0:T(8,128)(2,1)S(1)}, u32[]{:S(2)}, u32[]{:S(2)}) collective-permute-start(bf16[64,256]{1,0:T(8,128)(2,1)S(1)} %get-tuple-element.7), channel_id=1, source_target_pairs={{0,1},{2,3},{4,5},{6,7},{8,9},{10,11},{12,13},{14,15},{16,17},{18,... | collective-permute-start | bytes 98312 | tf_op jit(solution)/shard_map/ppermute | solution.py:18
  128.9 1.3 collective-permute-start.5
  130.2 1.8 collective-permute-done.5
  132.0 0.2 copy_bitcast_fusion.1
  132.1 3.0 %gather_fusion.2 = bf16[256,64,128]{2,1,0:T(8,128)(2,1)} fusion(bf16[64,36,128]{2,0,1:T(8,128)(2,1)S(1)} %copy_bitcast_fusion.1, s32[1024]{0:T(1024)S(1)} %pad_clamp_fusion), kind=kCustom, calls=%fused_computation.2 | custom fusion | bytes 8389632 | tf_op jit(solution)/shard_map/gather | solution.py:29
  135.2 7.6 %fusion.14 = f32[32,64,128,1]{2,1,3,0:T(8,128)S(1)} fusion(bf16[64,32,8,128]{3,0,2,1:T(8,128)(2,1)} %bitcast.119, bf16[32,8,128,128]{3,2,1,0:T(8,128)(2,1)} %param.6), kind=kOutput, calls=%fused_computation.38 | convolution fusion | flops 536870912 | bytes 13631488 | tf_op jit(solution)/shard_map/rjab,krjb->kra/dot_general | solution.py:30
  142.8 0.5 fusion.4
  143.3 0.5 copy-done.4
  143.8 2.1 %collective-permute-start.6 = (bf16[64,256]{1,0:T(8,128)(2,1)S(1)}, bf16[64,256]{1,0:T(8,128)(2,1)S(1)}, u32[]{:S(2)}, u32[]{:S(2)}) collective-permute-start(bf16[64,256]{1,0:T(8,128)(2,1)S(1)} %get-tuple-element.5), channel_id=1, source_target_pairs={{0,1},{2,3},{4,5},{6,7},{8,9},{10,11},{12,13},{14,15},{16,17},{18,... | collective-permute-start | bytes 98312 | tf_op jit(solution)/shard_map/ppermute | solution.py:18
  145.9 1.5 collective-permute-start.7
  147.4 1.6 copy.24
  149.0 2.6 %reshape.50 = f32[64,16,256]{2,1,0:T(8,128)} reshape(f32[64,32,128]{2,1,0:T(8,128)} %copy.24) | data formatting | bytes 2097152 | tf_op jit(solution)/shard_map/reshape | solution.py:31
  151.6 1.6 copy.26
  153.2 1.5 reshape.49
  154.7 1.6 copy.28
  156.3 2.5 %reshape.48 = f32[64,16,256]{2,1,0:T(8,128)} reshape(f32[64,32,128]{2,1,0:T(8,128)} %copy.28) | data formatting | bytes 2097152 | tf_op jit(solution)/shard_map/reshape | solution.py:31
  158.9 0.2 copy_bitcast_fusion
  159.0 3.0 %gather_fusion.3 = bf16[256,64,128]{2,1,0:T(8,128)(2,1)} fusion(bf16[64,36,128]{2,0,1:T(8,128)(2,1)S(1)} %copy_bitcast_fusion, s32[1024]{0:T(1024)S(1)} %pad_clamp_fusion), kind=kCustom, calls=%fused_computation.3 | custom fusion | bytes 8389632 | tf_op jit(solution)/shard_map/gather | solution.py:29
  162.1 7.6 %convolution_bitcast_fusion = f32[64,32,128]{2,0,1:T(8,128)S(1)} fusion(bf16[64,32,8,128]{3,0,2,1:T(8,128)(2,1)} %bitcast.116, bf16[32,8,128,128]{3,2,1,0:T(8,128)(2,1)} %param.6), kind=kOutput, calls=%fused_computation.4 | convolution fusion | flops 536870912 | bytes 13631488 | tf_op jit(solution)/shard_map/rjab,krjb->kra/dot_general | solution.py:30
  169.7 1.6 copy.30
  171.3 2.5 %reshape.47 = f32[64,16,256]{2,1,0:T(8,128)} reshape(f32[64,32,128]{2,1,0:T(8,128)} %copy.30) | data formatting | bytes 2097152 | tf_op jit(solution)/shard_map/reshape | solution.py:31
  173.8 2.4 %subtract_convert_fusion = bf16[64,16,256]{2,1,0:T(8,128)(2,1)S(1)} fusion(f32[64,16,256]{2,1,0:T(8,128)} %reshape.47, f32[64,16,256]{2,1,0:T(8,128)} %reshape.48, f32[64,16,256]{2,1,0:T(8,128)S(1)} %reshape.49, f32[64,16,256]{2,1,0:T(8,128)S(1)} %copy-done.8, bf16[16,64,256]{2,1,0:T(8,128)(2,1)S(1)} %copy-done.7), kind=kLoop, calls=%fused_computation.18 | loop fusion | flops 4456448 | bytes 5242880 | tf_op jit(solution)/shard_map/convert_element_type | solution.py:45
  176.2 0.2 copy.34
  176.3 19.0 %all_to_all.35 = bf16[64,16,256]{2,0,1:T(8,128)(2,1)S(1)} all-to-all(bf16[64,16,256]{2,0,1:T(8,128)(2,1)S(1)} %copy.34), channel_id=1, replica_groups=mesh['vec'=16,'row'=2] {'vec'}, dimensions={1} | all-to-all | bytes 1048576 | tf_op jit(solution)/shard_map/all_to_all | solution.py:60
  195.3 1.0 copy.35
  (34 shorter events, 0.1 us)
Async XLA Ops:
  6.5 66.7 %copy-start = (bf16[1,256,1024]{2,1,0:T(8,128)(2,1)S(1)}, bf16[1,256,1024]{2,1,0:T(8,128)(2,1)}, u32[]{:S(2)}) copy-start(bf16[1,256,1024]{2,1,0:T(8,128)(2,1)} %param.4) | copy-start | bytes 1572868
  6.5 74.3 %copy-start.11 = (s32[32,8]{0,1:T(8,128)S(1)}, s32[32,8]{0,1:T(8,128)}, u32[]{:S(2)}) copy-start(s32[32,8]{0,1:T(8,128)} %param.7) | copy-start | bytes 3076
  6.5 66.7 %all-gather.2.cloned.1.call-start = ((), (), s32[]{:S(2)}) async-start(), calls=%async_computation.2 | async-start | bytes 2228224 | tf_op jit(solution)/shard_map/all_gather | solution.py:53
  76.4 18.6 %all-to-all-start = ((bf16[16,64,256]{2,1,0:T(8,128)(2,1)}), bf16[16,64,256]{2,1,0:T(8,128)(2,1)S(1)}, u32[]{:S(2)}, u32[]{:S(2)}) async-start(bf16[16,64,256]{2,1,0:T(8,128)(2,1)} %bitcast.1), calls=%async_computation | async-start | bytes 1048576 | tf_op jit(solution)/shard_map/all_to_all | solution.py:58
  95.0 2.7 %copy-start.6 = (bf16[16,64,256]{2,1,0:T(8,128)(2,1)}, bf16[16,64,256]{2,1,0:T(8,128)(2,1)S(1)}, u32[]{:S(2)}) copy-start(bf16[16,64,256]{2,1,0:T(8,128)(2,1)S(1)} %all-to-all-done) | copy-start | bytes 1572868
  95.0 15.2 %copy-start.1 = (bf16[8,8,16,256]{3,1,2,0:T(8,128)(2,1)}, bf16[8,8,16,256]{3,1,2,0:T(8,128)(2,1)S(1)}, u32[]{:S(2)}) copy-start(bf16[8,8,16,256]{3,1,2,0:T(8,128)(2,1)S(1)} %copy.47) | copy-start | bytes 1572868
  95.0 2.6 %collective-permute-start = (bf16[64,256]{1,0:T(8,128)(2,1)S(1)}, bf16[64,256]{1,0:T(8,128)(2,1)S(1)}, u32[]{:S(2)}, u32[]{:S(2)}) collective-permute-start(bf16[64,256]{1,0:T(8,128)(2,1)S(1)} %get-tuple-element.11), channel_id=1, source_target_pairs={{0,1},{2,3},{4,5},{6,7},{8,9},{10,11},{12,13},{14,15},{16,17},{18,... | collective-permute-start | bytes 98312 | tf_op jit(solution)/shard_map/ppermute | solution.py:18
  96.3 3.1 %collective-permute-start.1 = (bf16[64,256]{1,0:T(8,128)(2,1)S(1)}, bf16[64,256]{1,0:T(8,128)(2,1)S(1)}, u32[]{:S(2)}, u32[]{:S(2)}) collective-permute-start(bf16[64,256]{1,0:T(8,128)(2,1)S(1)} %get-tuple-element.12), channel_id=1, source_target_pairs={{1,0},{3,2},{5,4},{7,6},{9,8},{11,10},{13,12},{15,14},{17,16},{19,... | collective-permute-start | bytes 98312 | tf_op jit(solution)/shard_map/ppermute | solution.py:21
  110.5 3.4 %collective-permute-start.2 = (bf16[64,256]{1,0:T(8,128)(2,1)S(1)}, bf16[64,256]{1,0:T(8,128)(2,1)S(1)}, u32[]{:S(2)}, u32[]{:S(2)}) collective-permute-start(bf16[64,256]{1,0:T(8,128)(2,1)S(1)} %get-tuple-element.9), channel_id=1, source_target_pairs={{0,1},{2,3},{4,5},{6,7},{8,9},{10,11},{12,13},{14,15},{16,17},{18,... | collective-permute-start | bytes 98312 | tf_op jit(solution)/shard_map/ppermute | solution.py:18
  112.5 3.1 %collective-permute-start.3 = (bf16[64,256]{1,0:T(8,128)(2,1)S(1)}, bf16[64,256]{1,0:T(8,128)(2,1)S(1)}, u32[]{:S(2)}, u32[]{:S(2)}) collective-permute-start(bf16[64,256]{1,0:T(8,128)(2,1)S(1)} %get-tuple-element.10), channel_id=1, source_target_pairs={{1,0},{3,2},{5,4},{7,6},{9,8},{11,10},{13,12},{15,14},{17,16},{19,... | collective-permute-start | bytes 98312 | tf_op jit(solution)/shard_map/ppermute | solution.py:21
  118.8 7.7 %copy-start.2 = (bf16[8,8,16,256]{3,1,2,0:T(8,128)(2,1)S(1)}, bf16[8,8,16,256]{3,1,2,0:T(8,128)(2,1)}, u32[]{:S(2)}) copy-start(bf16[8,8,16,256]{3,1,2,0:T(8,128)(2,1)} %copy-done.1) | copy-start | bytes 1572868
  126.8 3.4 %collective-permute-start.4 = (bf16[64,256]{1,0:T(8,128)(2,1)S(1)}, bf16[64,256]{1,0:T(8,128)(2,1)S(1)}, u32[]{:S(2)}, u32[]{:S(2)}) collective-permute-start(bf16[64,256]{1,0:T(8,128)(2,1)S(1)} %get-tuple-element.7), channel_id=1, source_target_pairs={{0,1},{2,3},{4,5},{6,7},{8,9},{10,11},{12,13},{14,15},{16,17},{18,... | collective-permute-start | bytes 98312 | tf_op jit(solution)/shard_map/ppermute | solution.py:18
  128.9 3.1 %collective-permute-start.5 = (bf16[64,256]{1,0:T(8,128)(2,1)S(1)}, bf16[64,256]{1,0:T(8,128)(2,1)S(1)}, u32[]{:S(2)}, u32[]{:S(2)}) collective-permute-start(bf16[64,256]{1,0:T(8,128)(2,1)S(1)} %get-tuple-element.8), channel_id=1, source_target_pairs={{1,0},{3,2},{5,4},{7,6},{9,8},{11,10},{13,12},{15,14},{17,16},{19,... | collective-permute-start | bytes 98312 | tf_op jit(solution)/shard_map/ppermute | solution.py:21
  135.2 7.7 %copy-start.3 = (bf16[8,8,16,256]{3,1,2,0:T(8,128)(2,1)S(1)}, bf16[8,8,16,256]{3,1,2,0:T(8,128)(2,1)}, u32[]{:S(2)}) copy-start(bf16[8,8,16,256]{3,1,2,0:T(8,128)(2,1)} %copy-done.1) | copy-start | bytes 1572868
  142.8 1.0 copy-start.4
  143.8 3.6 %copy-start.9 = (bf16[64,4096]{1,0:T(8,128)(2,1)}, bf16[64,4096]{1,0:T(8,128)(2,1)S(1)}, u32[]{:S(2)}) copy-start(bf16[64,4096]{1,0:T(8,128)(2,1)S(1)} %fusion.4) | copy-start | bytes 1572868
  143.8 15.0 %collective-permute-start.6 = (bf16[64,256]{1,0:T(8,128)(2,1)S(1)}, bf16[64,256]{1,0:T(8,128)(2,1)S(1)}, u32[]{:S(2)}, u32[]{:S(2)}) collective-permute-start(bf16[64,256]{1,0:T(8,128)(2,1)S(1)} %get-tuple-element.5), channel_id=1, source_target_pairs={{0,1},{2,3},{4,5},{6,7},{8,9},{10,11},{12,13},{14,15},{16,17},{18,... | collective-permute-start | bytes 98312 | tf_op jit(solution)/shard_map/ppermute | solution.py:18
  145.9 12.9 %collective-permute-start.7 = (bf16[64,256]{1,0:T(8,128)(2,1)S(1)}, bf16[64,256]{1,0:T(8,128)(2,1)S(1)}, u32[]{:S(2)}, u32[]{:S(2)}) collective-permute-start(bf16[64,256]{1,0:T(8,128)(2,1)S(1)} %get-tuple-element.6), channel_id=1, source_target_pairs={{1,0},{3,2},{5,4},{7,6},{9,8},{11,10},{13,12},{15,14},{17,16},{19,... | collective-permute-start | bytes 98312 | tf_op jit(solution)/shard_map/ppermute | solution.py:21
  149.0 5.7 %copy-start.5 = (f32[32,64,128,1]{2,1,3,0:T(8,128)S(1)}, f32[32,64,128,1]{2,1,3,0:T(8,128)}, u32[]{:S(2)}) copy-start(f32[32,64,128,1]{2,1,3,0:T(8,128)} %copy-done.4) | copy-start | bytes 3145732
  151.6 7.2 %copy-start.10 = (bf16[64,4096]{1,0:T(8,128)(2,1)S(1)}, bf16[64,4096]{1,0:T(8,128)(2,1)}, u32[]{:S(2)}) copy-start(bf16[64,4096]{1,0:T(8,128)(2,1)} %copy-done.9) | copy-start | bytes 1572868
  169.7 4.1 %copy-start.7 = (bf16[16,64,256]{2,1,0:T(8,128)(2,1)S(1)}, bf16[16,64,256]{2,1,0:T(8,128)(2,1)}, u32[]{:S(2)}) copy-start(bf16[16,64,256]{2,1,0:T(8,128)(2,1)} %copy-done.6) | copy-start | bytes 1572868
  169.7 4.1 %copy-start.8 = (f32[64,16,256]{2,1,0:T(8,128)S(1)}, f32[64,16,256]{2,1,0:T(8,128)}, u32[]{:S(2)}) copy-start(f32[64,16,256]{2,1,0:T(8,128)} %reshape.50) | copy-start | bytes 3145732
Sparse Core Ops, SparseCore 0:
  10.1 63.0 all-gather.1
where the time goes:
time: 204 us; the launch traced here: 203 us
  waiting for transfers between devices  86 us (42%)
  matrix products  33.6 us (16%)
  local copies, waits for them, and re-layouts  29.7 us (15%)
  blocking collectives  19 us (9%)
  starting transfers between devices  17.3 us (8%)
  between operations  13.7 us (7%)
  other arithmetic  3.9 us (2%)
    all_gather x1, waiting for transfers between devices, local(): lax.all_gather(rotation, 'vec', axis=1, tiled=True)  66 us
    dot_general x4, matrix products, apply_matrix(): jnp.einsum('rjab,krjb->kra', blocks, picked, preferred_element_type=jnp.f...  30.5 us
    all_to_all x1, blocking collectives, local(): lax.all_to_all(filtered, 'vec', split_axis=1, concat_axis=0, tiled=True)  19 us
    all_to_all x1, waiting for transfers between devices, local(): lax.all_to_all(rotated, 'vec', split_axis=0, concat_axis=1, tiled=True)  14 us
    gather x4, local copies, waits for them, and re-layouts, apply_matrix(): picked = stacked[:, offsets]  12.2 us
    reshape x4, local copies, waits for them, and re-layouts, apply_matrix(): return product.reshape(extended.shape[0], -1)  9.18 us
    ppermute x4, starting transfers between devices, with_halo(): lax.ppermute(lax.slice_in_dim(block, block.shape[dim] - width, None, axis...  7.49 us
    transpose x4, local copies, waits for them, and re-layouts, apply_matrix(): jnp.einsum('rjab,krjb->kra', blocks, picked, preferred_element_type=jnp.f...  6.33 us
  transfers between devices with their start and end apart: 10, of which 5 were waited for; matrix products, arithmetic and copies ran while one was open for 6% of the time, Pallas kernels for 0%

commit v1 on v0

--- a/solution.py
+++ b/solution.py
@@ -1,3 +1,4 @@
+import functools
 import jax
 import jax.numpy as jnp
 from jax import lax
@@ -8,6 +9,33 @@
 STEPS = 4
 centre = 0.3
 half_width = 1.2
+
+
+def apply_waves_in(u, along_axis):
+    y1, out_arr, local_part = (lax.axis_size(along_axis), lax.axis_index(along_axis), u.shape[1])
+    seen_now = lax.dynamic_update_slice_in_dim(
+        jnp.zeros(
+            [hop_no * y1 if no == 1 else hop_no for no, hop_no in enumerate(u.shape)], u.dtype
+        ),
+        u,
+        out_arr * local_part,
+        axis=1,
+    )
+    state_next = t1 = u
+    for to_i in [*range(1, y1 // 2 + 1)]:
+        state_next = lax.ppermute(state_next, along_axis, [(no, (no + 1) % y1) for no in range(y1)])
+        seen_now = lax.dynamic_update_slice_in_dim(
+            seen_now, state_next, (out_arr - to_i) % y1 * local_part, axis=1
+        )
+        if 2 * to_i < y1:
+            t1 = lax.ppermute(t1, along_axis, [(no, (no - 1) % y1) for no in range(y1)])
+            seen_now = lax.dynamic_update_slice_in_dim(
+                seen_now, t1, (out_arr + to_i) % y1 * local_part, axis=1
+            )
+    return seen_now
+
+
+cut_the_block = functools.partial(apply_waves_in, along_axis="vec")
 
 
 def with_halo(block, sides, width):
@@ -50,10 +78,7 @@
     offsets = column_blocks - (lax.axis_index("row") * column_blocks.shape[0] - HB)
     contract = (((0,), (1,)), ((), ()))
     rotated = lax.dot_general(
-        lax.all_gather(rotation, "vec", axis=1, tiled=True),
-        local_rows,
-        contract,
-        preferred_element_type=jnp.float32,
+        cut_the_block(rotation), local_rows, contract, preferred_element_type=jnp.float32
     ).astype(jnp.bfloat16)
     vec_panel = lax.all_to_all(rotated, "vec", split_axis=0, concat_axis=1, tiled=True)
     filtered = filter_panel(vec_panel, blocks, offsets)

time: 204 us -> 191 us (0.936)
  starting transfers between devices: 17.3 us -> 57.7 us
  waiting for transfers between devices: 86 us -> 46.6 us
  between operations: 13.7 us -> 0.49 us
    all_gather x1 -> x0, waiting for transfers between devices: 66 us -> none  [local(): lax.all_gather(rotation, 'vec', axis=1, tiled=True)]
    ppermute x0 -> x15, starting transfers between devices: none -> 41.3 us  [the longest x7 38.3 us: apply_waves_in(): t1 = lax.ppermute(t1, along_axis, [(no, (no - 1) % y1) for no in range(y1)])]
    ppermute x0 -> x15, waiting for transfers between devices: none -> 30.7 us  [the longest x8 30.5 us: apply_waves_in(): lax.ppermute(state_next, along_axis, [(no, (no + 1) % y1) for no in range...]
    all_to_all x1, waiting for transfers between devices: 14 us -> 10.5 us  [local(): lax.all_to_all(rotated, 'vec', split_axis=0, concat_axis=1, tiled=True)]
  transfers between devices with their start and end apart: 10 -> 24, of which waited for: 5 -> 13; matrix products, arithmetic and copies ran while one was open for 6% -> 6% of each run, Pallas kernels for 0% -> 0%
where the time goes in v1:
time: 191 us
  starting transfers between devices  57.7 us (30%)
  waiting for transfers between devices  46.6 us (24%)
  matrix products  32 us (17%)
  local copies, waits for them, and re-layouts  30.9 us (16%)
  blocking collectives  19.1 us (10%)
  other arithmetic  3.9 us (2%)
    ppermute x7, starting transfers between devices, apply_waves_in(): t1 = lax.ppermute(t1, along_axis, [(no, (no - 1) % y1) for no in range(y1)])  38.3 us
    dot_general x4, matrix products, apply_matrix(): jnp.einsum('rjab,krjb->kra', blocks, picked, preferred_element_type=jnp.f...  30.5 us
    ppermute x8, waiting for transfers between devices, apply_waves_in(): lax.ppermute(state_next, along_axis, [(no, (no + 1) % y1) for no in range...  30.5 us
    all_to_all x1, blocking collectives, local(): lax.all_to_all(filtered, 'vec', split_axis=1, concat_axis=0, tiled=True)  19.1 us
    gather x4, local copies, waits for them, and re-layouts, apply_matrix(): picked = stacked[:, offsets]  12.3 us
    all_to_all x1, waiting for transfers between devices, local(): lax.all_to_all(rotated, 'vec', split_axis=0, concat_axis=1, tiled=True)  10.5 us
    reshape x4, local copies, waits for them, and re-layouts, apply_matrix(): return product.reshape(extended.shape[0], -1)  9.09 us
    ppermute x4, starting transfers between devices, with_halo(): lax.ppermute(lax.slice_in_dim(block, block.shape[dim] - width, None, axis...  7.48 us
  transfers between devices with their start and end apart: 24, of which 13 were waited for; matrix products, arithmetic and copies ran while one was open for 6% of the time, Pallas kernels for 0%

profile of v1, /device:TPU:0, one launch (start us, length us, event | category | flops | bytes accessed | tf_op | source)
XLA Modules:
  0.0 190.8 jit_solution(6429857822969243766)
XLA Ops:
  0.0 3.0 %collective-permute-start = (bf16[1024,64]{0,1:T(8,128)(2,1)}, bf16[1024,64]{0,1:T(8,128)(2,1)S(1)}, u32[]{:S(2)}, u32[]{:S(2)}) collective-permute-start(bf16[1024,64]{0,1:T(8,128)(2,1)} %param.5), channel_id=1, source_target_pairs={{0,2},{2,4},{4,6},{6,8},{8,10},{10,12},{12,14},{14,16},{16,18},{18... | collective-permute-start | bytes 393224 | tf_op jit(solution)/shard_map/ppermute | solution.py:26
  3.0 4.1 %collective-permute-start.1 = (bf16[1024,64]{0,1:T(8,128)(2,1)}, bf16[1024,64]{0,1:T(8,128)(2,1)S(1)}, u32[]{:S(2)}, u32[]{:S(2)}) collective-permute-start(bf16[1024,64]{0,1:T(8,128)(2,1)} %param.5), channel_id=1, source_target_pairs={{0,30},{2,0},{4,2},{6,4},{8,6},{10,8},{12,10},{14,12},{16,14},{18,... | collective-permute-start | bytes 393224 | tf_op jit(solution)/shard_map/ppermute | solution.py:31
  7.3 3.5 %collective-permute-done = bf16[1024,64]{0,1:T(8,128)(2,1)S(1)} collective-permute-done((bf16[1024,64]{0,1:T(8,128)(2,1)}, bf16[1024,64]{0,1:T(8,128)(2,1)S(1)}, u32[]{:S(2)}, u32[]{:S(2)}) %collective-permute-start) | collective-permute-done | bytes 131104 | tf_op jit(solution)/shard_map/ppermute | solution.py:26
  11.0 5.4 %collective-permute-start.3 = (bf16[1024,64]{0,1:T(8,128)(2,1)S(1)}, bf16[1024,64]{0,1:T(8,128)(2,1)S(1)}, u32[]{:S(2)}, u32[]{:S(2)}) collective-permute-start(bf16[1024,64]{0,1:T(8,128)(2,1)S(1)} %collective-permute-done.1), channel_id=1, source_target_pairs={{0,30},{2,0},{4,2},{6,4},{8,6},{10,8},{12,10},{14,12},{16,14},{18,... | collective-permute-start | bytes 393224 | tf_op jit(solution)/shard_map/ppermute | solution.py:31
  16.5 2.9 %collective-permute-done.2 = bf16[1024,64]{0,1:T(8,128)(2,1)S(1)} collective-permute-done((bf16[1024,64]{0,1:T(8,128)(2,1)S(1)}, bf16[1024,64]{0,1:T(8,128)(2,1)S(1)}, u32[]{:S(2)}, u32[]{:S(2)}) %collective-permute-start.2) | collective-permute-done | bytes 131104 | tf_op jit(solution)/shard_map/ppermute | solution.py:26
  19.4 5.7 %collective-permute-start.5 = (bf16[1024,64]{0,1:T(8,128)(2,1)S(1)}, bf16[1024,64]{0,1:T(8,128)(2,1)S(1)}, u32[]{:S(2)}, u32[]{:S(2)}) collective-permute-start(bf16[1024,64]{0,1:T(8,128)(2,1)S(1)} %collective-permute-done.3), channel_id=1, source_target_pairs={{0,30},{2,0},{4,2},{6,4},{8,6},{10,8},{12,10},{14,12},{16,14},{18,... | collective-permute-start | bytes 393224 | tf_op jit(solution)/shard_map/ppermute | solution.py:31
  25.1 2.9 %collective-permute-done.4 = bf16[1024,64]{0,1:T(8,128)(2,1)S(1)} collective-permute-done((bf16[1024,64]{0,1:T(8,128)(2,1)S(1)}, bf16[1024,64]{0,1:T(8,128)(2,1)S(1)}, u32[]{:S(2)}, u32[]{:S(2)}) %collective-permute-start.4) | collective-permute-done | bytes 131104 | tf_op jit(solution)/shard_map/ppermute | solution.py:26
  28.0 5.7 %collective-permute-start.7 = (bf16[1024,64]{0,1:T(8,128)(2,1)S(1)}, bf16[1024,64]{0,1:T(8,128)(2,1)S(1)}, u32[]{:S(2)}, u32[]{:S(2)}) collective-permute-start(bf16[1024,64]{0,1:T(8,128)(2,1)S(1)} %collective-permute-done.5), channel_id=1, source_target_pairs={{0,30},{2,0},{4,2},{6,4},{8,6},{10,8},{12,10},{14,12},{16,14},{18,... | collective-permute-start | bytes 393224 | tf_op jit(solution)/shard_map/ppermute | solution.py:31
  33.8 2.9 %collective-permute-done.6 = bf16[1024,64]{0,1:T(8,128)(2,1)S(1)} collective-permute-done((bf16[1024,64]{0,1:T(8,128)(2,1)S(1)}, bf16[1024,64]{0,1:T(8,128)(2,1)S(1)}, u32[]{:S(2)}, u32[]{:S(2)}) %collective-permute-start.6) | collective-permute-done | bytes 131104 | tf_op jit(solution)/shard_map/ppermute | solution.py:26
  36.7 5.6 %collective-permute-start.9 = (bf16[1024,64]{0,1:T(8,128)(2,1)S(1)}, bf16[1024,64]{0,1:T(8,128)(2,1)S(1)}, u32[]{:S(2)}, u32[]{:S(2)}) collective-permute-start(bf16[1024,64]{0,1:T(8,128)(2,1)S(1)} %collective-permute-done.7), channel_id=1, source_target_pairs={{0,30},{2,0},{4,2},{6,4},{8,6},{10,8},{12,10},{14,12},{16,14},{18,... | collective-permute-start | bytes 393224 | tf_op jit(solution)/shard_map/ppermute | solution.py:31
  42.4 2.9 %collective-permute-done.8 = bf16[1024,64]{0,1:T(8,128)(2,1)S(1)} collective-permute-done((bf16[1024,64]{0,1:T(8,128)(2,1)S(1)}, bf16[1024,64]{0,1:T(8,128)(2,1)S(1)}, u32[]{:S(2)}, u32[]{:S(2)}) %collective-permute-start.8) | collective-permute-done | bytes 131104 | tf_op jit(solution)/shard_map/ppermute | solution.py:26
  45.3 5.7 %collective-permute-start.11 = (bf16[1024,64]{0,1:T(8,128)(2,1)S(1)}, bf16[1024,64]{0,1:T(8,128)(2,1)S(1)}, u32[]{:S(2)}, u32[]{:S(2)}) collective-permute-start(bf16[1024,64]{0,1:T(8,128)(2,1)S(1)} %collective-permute-done.9), channel_id=1, source_target_pairs={{0,30},{2,0},{4,2},{6,4},{8,6},{10,8},{12,10},{14,12},{16,14},{18,... | collective-permute-start | bytes 393224 | tf_op jit(solution)/shard_map/ppermute | solution.py:31
  51.0 3.1 %collective-permute-done.10 = bf16[1024,64]{0,1:T(8,128)(2,1)S(1)} collective-permute-done((bf16[1024,64]{0,1:T(8,128)(2,1)S(1)}, bf16[1024,64]{0,1:T(8,128)(2,1)S(1)}, u32[]{:S(2)}, u32[]{:S(2)}) %collective-permute-start.10) | collective-permute-done | bytes 131104 | tf_op jit(solution)/shard_map/ppermute | solution.py:26
  54.1 6.1 %collective-permute-start.13 = (bf16[1024,64]{0,1:T(8,128)(2,1)S(1)}, bf16[1024,64]{0,1:T(8,128)(2,1)S(1)}, u32[]{:S(2)}, u32[]{:S(2)}) collective-permute-start(bf16[1024,64]{0,1:T(8,128)(2,1)S(1)} %collective-permute-done.11), channel_id=1, source_target_pairs={{0,30},{2,0},{4,2},{6,4},{8,6},{10,8},{12,10},{14,12},{16,14},{18,... | collective-permute-start | bytes 393224 | tf_op jit(solution)/shard_map/ppermute | solution.py:31
  60.2 3.8 %collective-permute-done.12 = bf16[1024,64]{0,1:T(8,128)(2,1)S(1)} collective-permute-done((bf16[1024,64]{0,1:T(8,128)(2,1)S(1)}, bf16[1024,64]{0,1:T(8,128)(2,1)S(1)}, u32[]{:S(2)}, u32[]{:S(2)}) %collective-permute-start.12) | collective-permute-done | bytes 131104 | tf_op jit(solution)/shard_map/ppermute | solution.py:26
  64.0 8.6 %collective-permute-done.14 = bf16[1024,64]{0,1:T(8,128)(2,1)S(1)} collective-permute-done((bf16[1024,64]{0,1:T(8,128)(2,1)S(1)}, bf16[1024,64]{0,1:T(8,128)(2,1)S(1)}, u32[]{:S(2)}, u32[]{:S(2)}) %collective-permute-start.14) | collective-permute-done | bytes 131104 | tf_op jit(solution)/shard_map/ppermute | solution.py:26
  72.6 1.5 convolution_convert_fusion
  74.2 3.6 %all-to-all-start = ((bf16[16,64,256]{2,1,0:T(8,128)(2,1)}), bf16[16,64,256]{2,1,0:T(8,128)(2,1)S(1)}, u32[]{:S(2)}, u32[]{:S(2)}) async-start(bf16[16,64,256]{2,1,0:T(8,128)(2,1)} %bitcast.1), calls=%async_computation | async-start | bytes 1048576 | tf_op jit(solution)/shard_map/all_to_all | solution.py:83
  78.0 10.5 %all-to-all-done = bf16[16,64,256]{2,1,0:T(8,128)(2,1)S(1)} async-done(((bf16[16,64,256]{2,1,0:T(8,128)(2,1)}), bf16[16,64,256]{2,1,0:T(8,128)(2,1)S(1)}, u32[]{:S(2)}, u32[]{:S(2)}) %all-to-all-start) | async-done | bytes 524320 | tf_op jit(solution)/shard_map/all_to_all | solution.py:83
  88.6 1.3 collective-permute-start.15
  89.9 1.3 collective-permute-start.16
  91.2 1.8 collective-permute-done.16
  93.1 3.1 %gather_fusion = bf16[256,64,128]{2,1,0:T(8,128)(2,1)} fusion(bf16[64,36,128]{2,0,1:T(8,128)(2,1)S(1)} %copy_bitcast_fusion.3, s32[1024]{0:T(1024)S(1)} %pad_clamp_fusion), kind=kCustom, calls=%fused_computation | custom fusion | bytes 8389632 | tf_op jit(solution)/shard_map/gather | solution.py:57
  96.2 7.6 %fusion.12 = f32[32,64,128,1]{2,1,3,0:T(8,128)S(1)} fusion(bf16[64,32,8,128]{3,0,2,1:T(8,128)(2,1)} %bitcast.117, bf16[32,8,128,128]{3,2,1,0:T(8,128)(2,1)} %param.6), kind=kOutput, calls=%fused_computation.52 | convolution fusion | flops 536870912 | bytes 13631488 | tf_op jit(solution)/shard_map/rjab,krjb->kra/dot_general | solution.py:58
  104.0 2.1 %collective-permute-start.17 = (bf16[64,256]{1,0:T(8,128)(2,1)S(1)}, bf16[64,256]{1,0:T(8,128)(2,1)S(1)}, u32[]{:S(2)}, u32[]{:S(2)}) collective-permute-start(bf16[64,256]{1,0:T(8,128)(2,1)S(1)} %get-tuple-element.9), channel_id=1, source_target_pairs={{0,1},{2,3},{4,5},{6,7},{8,9},{10,11},{12,13},{14,15},{16,17},{18,... | collective-permute-start | bytes 98312 | tf_op jit(solution)/shard_map/ppermute | solution.py:46
  106.1 1.3 collective-permute-start.18
  107.4 1.8 collective-permute-done.18
  109.3 3.1 %gather_fusion.1 = bf16[256,64,128]{2,1,0:T(8,128)(2,1)} fusion(bf16[64,36,128]{2,0,1:T(8,128)(2,1)S(1)} %copy_bitcast_fusion.2, s32[1024]{0:T(1024)S(1)} %pad_clamp_fusion), kind=kCustom, calls=%fused_computation.1 | custom fusion | bytes 8389632 | tf_op jit(solution)/shard_map/gather | solution.py:57
  112.4 7.6 %fusion.13 = f32[32,64,128,1]{2,1,3,0:T(8,128)S(1)} fusion(bf16[64,32,8,128]{3,0,2,1:T(8,128)(2,1)} %bitcast.118, bf16[32,8,128,128]{3,2,1,0:T(8,128)(2,1)} %param.6), kind=kOutput, calls=%fused_computation.53 | convolution fusion | flops 536870912 | bytes 13631488 | tf_op jit(solution)/shard_map/rjab,krjb->kra/dot_general | solution.py:58
  120.4 2.1 %collective-permute-start.19 = (bf16[64,256]{1,0:T(8,128)(2,1)S(1)}, bf16[64,256]{1,0:T(8,128)(2,1)S(1)}, u32[]{:S(2)}, u32[]{:S(2)}) collective-permute-start(bf16[64,256]{1,0:T(8,128)(2,1)S(1)} %get-tuple-element.7), channel_id=1, source_target_pairs={{0,1},{2,3},{4,5},{6,7},{8,9},{10,11},{12,13},{14,15},{16,17},{18,... | collective-permute-start | bytes 98312 | tf_op jit(solution)/shard_map/ppermute | solution.py:46
  122.4 1.3 collective-permute-start.20
  123.7 1.8 collective-permute-done.20
  125.7 3.1 %gather_fusion.2 = bf16[256,64,128]{2,1,0:T(8,128)(2,1)} fusion(bf16[64,36,128]{2,0,1:T(8,128)(2,1)S(1)} %copy_bitcast_fusion.1, s32[1024]{0:T(1024)S(1)} %pad_clamp_fusion), kind=kCustom, calls=%fused_computation.2 | custom fusion | bytes 8389632 | tf_op jit(solution)/shard_map/gather | solution.py:57
  128.8 7.6 %fusion.14 = f32[32,64,128,1]{2,1,3,0:T(8,128)S(1)} fusion(bf16[64,32,8,128]{3,0,2,1:T(8,128)(2,1)} %bitcast.119, bf16[32,8,128,128]{3,2,1,0:T(8,128)(2,1)} %param.6), kind=kOutput, calls=%fused_computation.54 | convolution fusion | flops 536870912 | bytes 13631488 | tf_op jit(solution)/shard_map/rjab,krjb->kra/dot_general | solution.py:58
  138.2 2.1 %collective-permute-start.21 = (bf16[64,256]{1,0:T(8,128)(2,1)S(1)}, bf16[64,256]{1,0:T(8,128)(2,1)S(1)}, u32[]{:S(2)}, u32[]{:S(2)}) collective-permute-start(bf16[64,256]{1,0:T(8,128)(2,1)S(1)} %get-tuple-element.5), channel_id=1, source_target_pairs={{0,1},{2,3},{4,5},{6,7},{8,9},{10,11},{12,13},{14,15},{16,17},{18,... | collective-permute-start | bytes 98312 | tf_op jit(solution)/shard_map/ppermute | solution.py:46
  140.3 1.5 collective-permute-start.22
  141.8 1.6 copy.24
  143.3 2.5 %reshape.50 = f32[64,16,256]{2,1,0:T(8,128)} reshape(f32[64,32,128]{2,1,0:T(8,128)} %copy.24) | data formatting | bytes 2097152 | tf_op jit(solution)/shard_map/reshape | solution.py:59
  145.9 1.6 copy.26
  147.4 1.5 reshape.49
  149.0 1.6 copy.28
  150.6 2.5 %reshape.48 = f32[64,16,256]{2,1,0:T(8,128)} reshape(f32[64,32,128]{2,1,0:T(8,128)} %copy.28) | data formatting | bytes 2097152 | tf_op jit(solution)/shard_map/reshape | solution.py:59
  153.3 3.1 %gather_fusion.3 = bf16[256,64,128]{2,1,0:T(8,128)(2,1)} fusion(bf16[64,36,128]{2,0,1:T(8,128)(2,1)S(1)} %copy_bitcast_fusion, s32[1024]{0:T(1024)S(1)} %pad_clamp_fusion), kind=kCustom, calls=%fused_computation.3 | custom fusion | bytes 8389632 | tf_op jit(solution)/shard_map/gather | solution.py:57
  156.4 7.6 %convolution_bitcast_fusion = f32[64,32,128]{2,0,1:T(8,128)S(1)} fusion(bf16[64,32,8,128]{3,0,2,1:T(8,128)(2,1)} %bitcast.116, bf16[32,8,128,128]{3,2,1,0:T(8,128)(2,1)} %param.6), kind=kOutput, calls=%fused_computation.4 | convolution fusion | flops 536870912 | bytes 13631488 | tf_op jit(solution)/shard_map/rjab,krjb->kra/dot_general | solution.py:58
  164.0 1.6 copy.30
  165.6 2.5 %reshape.47 = f32[64,16,256]{2,1,0:T(8,128)} reshape(f32[64,32,128]{2,1,0:T(8,128)} %copy.30) | data formatting | bytes 2097152 | tf_op jit(solution)/shard_map/reshape | solution.py:59
  168.1 2.4 %subtract_convert_fusion = bf16[64,16,256]{2,1,0:T(8,128)(2,1)S(1)} fusion(f32[64,16,256]{2,1,0:T(8,128)} %reshape.47, f32[64,16,256]{2,1,0:T(8,128)} %reshape.48, f32[64,16,256]{2,1,0:T(8,128)S(1)} %reshape.49, f32[64,16,256]{2,1,0:T(8,128)S(1)} %copy-done.8, bf16[16,64,256]{2,1,0:T(8,128)(2,1)S(1)} %copy-done.7), kind=kLoop, calls=%fused_computation.18 | loop fusion | flops 4456448 | bytes 5242880 | tf_op jit(solution)/shard_map/convert_element_type | solution.py:73
  170.6 19.1 %all_to_all.35 = bf16[64,16,256]{2,0,1:T(8,128)(2,1)S(1)} all-to-all(bf16[64,16,256]{2,0,1:T(8,128)(2,1)S(1)} %copy.34), channel_id=1, replica_groups=mesh['vec'=16,'row'=2] {'vec'}, dimensions={1} | all-to-all | bytes 1048576 | tf_op jit(solution)/shard_map/all_to_all | solution.py:85
  (80 shorter events, 5.0 us)
Async XLA Ops:
  0.0 72.6 %copy-start = (bf16[1,256,1024]{2,1,0:T(8,128)(2,1)S(1)}, bf16[1,256,1024]{2,1,0:T(8,128)(2,1)}, u32[]{:S(2)}) copy-start(bf16[1,256,1024]{2,1,0:T(8,128)(2,1)} %param.4) | copy-start | bytes 1572868
  0.0 7.3 %copy-start.11 = (bf16[1024,64]{0,1:T(8,128)(2,1)S(1)}, bf16[1024,64]{0,1:T(8,128)(2,1)}, u32[]{:S(2)}) copy-start(bf16[1024,64]{0,1:T(8,128)(2,1)} %param.5) | copy-start | bytes 393220
  0.0 10.8 %collective-permute-start = (bf16[1024,64]{0,1:T(8,128)(2,1)}, bf16[1024,64]{0,1:T(8,128)(2,1)S(1)}, u32[]{:S(2)}, u32[]{:S(2)}) collective-permute-start(bf16[1024,64]{0,1:T(8,128)(2,1)} %param.5), channel_id=1, source_target_pairs={{0,2},{2,4},{4,6},{6,8},{8,10},{10,12},{12,14},{14,16},{16,18},{18... | collective-permute-start | bytes 393224 | tf_op jit(solution)/shard_map/ppermute | solution.py:26
  3.0 8.1 %collective-permute-start.1 = (bf16[1024,64]{0,1:T(8,128)(2,1)}, bf16[1024,64]{0,1:T(8,128)(2,1)S(1)}, u32[]{:S(2)}, u32[]{:S(2)}) collective-permute-start(bf16[1024,64]{0,1:T(8,128)(2,1)} %param.5), channel_id=1, source_target_pairs={{0,30},{2,0},{4,2},{6,4},{8,6},{10,8},{12,10},{14,12},{16,14},{18,... | collective-permute-start | bytes 393224 | tf_op jit(solution)/shard_map/ppermute | solution.py:31
  10.8 8.6 %collective-permute-start.2 = (bf16[1024,64]{0,1:T(8,128)(2,1)S(1)}, bf16[1024,64]{0,1:T(8,128)(2,1)S(1)}, u32[]{:S(2)}, u32[]{:S(2)}) collective-permute-start(bf16[1024,64]{0,1:T(8,128)(2,1)S(1)} %collective-permute-done), channel_id=1, source_target_pairs={{0,2},{2,4},{4,6},{6,8},{8,10},{10,12},{12,14},{14,16},{16,18},{18... | collective-permute-start | bytes 393224 | tf_op jit(solution)/shard_map/ppermute | solution.py:26
  11.0 8.3 %collective-permute-start.3 = (bf16[1024,64]{0,1:T(8,128)(2,1)S(1)}, bf16[1024,64]{0,1:T(8,128)(2,1)S(1)}, u32[]{:S(2)}, u32[]{:S(2)}) collective-permute-start(bf16[1024,64]{0,1:T(8,128)(2,1)S(1)} %collective-permute-done.1), channel_id=1, source_target_pairs={{0,30},{2,0},{4,2},{6,4},{8,6},{10,8},{12,10},{14,12},{16,14},{18,... | collective-permute-start | bytes 393224 | tf_op jit(solution)/shard_map/ppermute | solution.py:31
  19.4 8.7 %collective-permute-start.4 = (bf16[1024,64]{0,1:T(8,128)(2,1)S(1)}, bf16[1024,64]{0,1:T(8,128)(2,1)S(1)}, u32[]{:S(2)}, u32[]{:S(2)}) collective-permute-start(bf16[1024,64]{0,1:T(8,128)(2,1)S(1)} %collective-permute-done.2), channel_id=1, source_target_pairs={{0,2},{2,4},{4,6},{6,8},{8,10},{10,12},{12,14},{14,16},{16,18},{18... | collective-permute-start | bytes 393224 | tf_op jit(solution)/shard_map/ppermute | solution.py:26
  19.4 8.7 %collective-permute-start.5 = (bf16[1024,64]{0,1:T(8,128)(2,1)S(1)}, bf16[1024,64]{0,1:T(8,128)(2,1)S(1)}, u32[]{:S(2)}, u32[]{:S(2)}) collective-permute-start(bf16[1024,64]{0,1:T(8,128)(2,1)S(1)} %collective-permute-done.3), channel_id=1, source_target_pairs={{0,30},{2,0},{4,2},{6,4},{8,6},{10,8},{12,10},{14,12},{16,14},{18,... | collective-permute-start | bytes 393224 | tf_op jit(solution)/shard_map/ppermute | solution.py:31
  28.0 8.7 %collective-permute-start.6 = (bf16[1024,64]{0,1:T(8,128)(2,1)S(1)}, bf16[1024,64]{0,1:T(8,128)(2,1)S(1)}, u32[]{:S(2)}, u32[]{:S(2)}) collective-permute-start(bf16[1024,64]{0,1:T(8,128)(2,1)S(1)} %collective-permute-done.4), channel_id=1, source_target_pairs={{0,2},{2,4},{4,6},{6,8},{8,10},{10,12},{12,14},{14,16},{16,18},{18... | collective-permute-start | bytes 393224 | tf_op jit(solution)/shard_map/ppermute | solution.py:26
  28.0 8.7 %collective-permute-start.7 = (bf16[1024,64]{0,1:T(8,128)(2,1)S(1)}, bf16[1024,64]{0,1:T(8,128)(2,1)S(1)}, u32[]{:S(2)}, u32[]{:S(2)}) collective-permute-start(bf16[1024,64]{0,1:T(8,128)(2,1)S(1)} %collective-permute-done.5), channel_id=1, source_target_pairs={{0,30},{2,0},{4,2},{6,4},{8,6},{10,8},{12,10},{14,12},{16,14},{18,... | collective-permute-start | bytes 393224 | tf_op jit(solution)/shard_map/ppermute | solution.py:31
  36.7 8.6 %collective-permute-start.8 = (bf16[1024,64]{0,1:T(8,128)(2,1)S(1)}, bf16[1024,64]{0,1:T(8,128)(2,1)S(1)}, u32[]{:S(2)}, u32[]{:S(2)}) collective-permute-start(bf16[1024,64]{0,1:T(8,128)(2,1)S(1)} %collective-permute-done.6), channel_id=1, source_target_pairs={{0,2},{2,4},{4,6},{6,8},{8,10},{10,12},{12,14},{14,16},{16,18},{18... | collective-permute-start | bytes 393224 | tf_op jit(solution)/shard_map/ppermute | solution.py:26
  36.7 8.6 %collective-permute-start.9 = (bf16[1024,64]{0,1:T(8,128)(2,1)S(1)}, bf16[1024,64]{0,1:T(8,128)(2,1)S(1)}, u32[]{:S(2)}, u32[]{:S(2)}) collective-permute-start(bf16[1024,64]{0,1:T(8,128)(2,1)S(1)} %collective-permute-done.7), channel_id=1, source_target_pairs={{0,30},{2,0},{4,2},{6,4},{8,6},{10,8},{12,10},{14,12},{16,14},{18,... | collective-permute-start | bytes 393224 | tf_op jit(solution)/shard_map/ppermute | solution.py:31
  45.3 8.8 %collective-permute-start.10 = (bf16[1024,64]{0,1:T(8,128)(2,1)S(1)}, bf16[1024,64]{0,1:T(8,128)(2,1)S(1)}, u32[]{:S(2)}, u32[]{:S(2)}) collective-permute-start(bf16[1024,64]{0,1:T(8,128)(2,1)S(1)} %collective-permute-done.8), channel_id=1, source_target_pairs={{0,2},{2,4},{4,6},{6,8},{8,10},{10,12},{12,14},{14,16},{16,18},{18... | collective-permute-start | bytes 393224 | tf_op jit(solution)/shard_map/ppermute | solution.py:26
  45.3 8.8 %collective-permute-start.11 = (bf16[1024,64]{0,1:T(8,128)(2,1)S(1)}, bf16[1024,64]{0,1:T(8,128)(2,1)S(1)}, u32[]{:S(2)}, u32[]{:S(2)}) collective-permute-start(bf16[1024,64]{0,1:T(8,128)(2,1)S(1)} %collective-permute-done.9), channel_id=1, source_target_pairs={{0,30},{2,0},{4,2},{6,4},{8,6},{10,8},{12,10},{14,12},{16,14},{18,... | collective-permute-start | bytes 393224 | tf_op jit(solution)/shard_map/ppermute | solution.py:31
  54.1 9.9 %collective-permute-start.12 = (bf16[1024,64]{0,1:T(8,128)(2,1)S(1)}, bf16[1024,64]{0,1:T(8,128)(2,1)S(1)}, u32[]{:S(2)}, u32[]{:S(2)}) collective-permute-start(bf16[1024,64]{0,1:T(8,128)(2,1)S(1)} %collective-permute-done.10), channel_id=1, source_target_pairs={{0,2},{2,4},{4,6},{6,8},{8,10},{10,12},{12,14},{14,16},{16,18},{18... | collective-permute-start | bytes 393224 | tf_op jit(solution)/shard_map/ppermute | solution.py:26
  54.1 9.9 %collective-permute-start.13 = (bf16[1024,64]{0,1:T(8,128)(2,1)S(1)}, bf16[1024,64]{0,1:T(8,128)(2,1)S(1)}, u32[]{:S(2)}, u32[]{:S(2)}) collective-permute-start(bf16[1024,64]{0,1:T(8,128)(2,1)S(1)} %collective-permute-done.11), channel_id=1, source_target_pairs={{0,30},{2,0},{4,2},{6,4},{8,6},{10,8},{12,10},{14,12},{16,14},{18,... | collective-permute-start | bytes 393224 | tf_op jit(solution)/shard_map/ppermute | solution.py:31
  64.0 8.6 %collective-permute-start.14 = (bf16[1024,64]{0,1:T(8,128)(2,1)S(1)}, bf16[1024,64]{0,1:T(8,128)(2,1)S(1)}, u32[]{:S(2)}, u32[]{:S(2)}) collective-permute-start(bf16[1024,64]{0,1:T(8,128)(2,1)S(1)} %collective-permute-done.12), channel_id=1, source_target_pairs={{0,2},{2,4},{4,6},{6,8},{8,10},{10,12},{12,14},{14,16},{16,18},{18... | collective-permute-start | bytes 393224 | tf_op jit(solution)/shard_map/ppermute | solution.py:26
  72.6 5.1 %copy-start.12 = (s32[32,8]{0,1:T(8,128)S(1)}, s32[32,8]{0,1:T(8,128)}, u32[]{:S(2)}) copy-start(s32[32,8]{0,1:T(8,128)} %param.7) | copy-start | bytes 3076
  74.2 14.3 %all-to-all-start = ((bf16[16,64,256]{2,1,0:T(8,128)(2,1)}), bf16[16,64,256]{2,1,0:T(8,128)(2,1)S(1)}, u32[]{:S(2)}, u32[]{:S(2)}) async-start(bf16[16,64,256]{2,1,0:T(8,128)(2,1)} %bitcast.1), calls=%async_computation | async-start | bytes 1048576 | tf_op jit(solution)/shard_map/all_to_all | solution.py:83
  88.5 2.7 %copy-start.6 = (bf16[16,64,256]{2,1,0:T(8,128)(2,1)}, bf16[16,64,256]{2,1,0:T(8,128)(2,1)S(1)}, u32[]{:S(2)}) copy-start(bf16[16,64,256]{2,1,0:T(8,128)(2,1)S(1)} %all-to-all-done) | copy-start | bytes 1572868
  88.5 15.3 %copy-start.1 = (bf16[8,8,16,256]{3,1,2,0:T(8,128)(2,1)}, bf16[8,8,16,256]{3,1,2,0:T(8,128)(2,1)S(1)}, u32[]{:S(2)}) copy-start(bf16[8,8,16,256]{3,1,2,0:T(8,128)(2,1)S(1)} %copy.47) | copy-start | bytes 1572868
  88.6 2.6 %collective-permute-start.15 = (bf16[64,256]{1,0:T(8,128)(2,1)S(1)}, bf16[64,256]{1,0:T(8,128)(2,1)S(1)}, u32[]{:S(2)}, u32[]{:S(2)}) collective-permute-start(bf16[64,256]{1,0:T(8,128)(2,1)S(1)} %get-tuple-element.11), channel_id=1, source_target_pairs={{0,1},{2,3},{4,5},{6,7},{8,9},{10,11},{12,13},{14,15},{16,17},{18,... | collective-permute-start | bytes 98312 | tf_op jit(solution)/shard_map/ppermute | solution.py:46
  89.9 3.1 %collective-permute-start.16 = (bf16[64,256]{1,0:T(8,128)(2,1)S(1)}, bf16[64,256]{1,0:T(8,128)(2,1)S(1)}, u32[]{:S(2)}, u32[]{:S(2)}) collective-permute-start(bf16[64,256]{1,0:T(8,128)(2,1)S(1)} %get-tuple-element.12), channel_id=1, source_target_pairs={{1,0},{3,2},{5,4},{7,6},{9,8},{11,10},{13,12},{15,14},{17,16},{19,... | collective-permute-start | bytes 98312 | tf_op jit(solution)/shard_map/ppermute | solution.py:49
  104.0 3.4 %collective-permute-start.17 = (bf16[64,256]{1,0:T(8,128)(2,1)S(1)}, bf16[64,256]{1,0:T(8,128)(2,1)S(1)}, u32[]{:S(2)}, u32[]{:S(2)}) collective-permute-start(bf16[64,256]{1,0:T(8,128)(2,1)S(1)} %get-tuple-element.9), channel_id=1, source_target_pairs={{0,1},{2,3},{4,5},{6,7},{8,9},{10,11},{12,13},{14,15},{16,17},{18,... | collective-permute-start | bytes 98312 | tf_op jit(solution)/shard_map/ppermute | solution.py:46
  106.1 3.1 %collective-permute-start.18 = (bf16[64,256]{1,0:T(8,128)(2,1)S(1)}, bf16[64,256]{1,0:T(8,128)(2,1)S(1)}, u32[]{:S(2)}, u32[]{:S(2)}) collective-permute-start(bf16[64,256]{1,0:T(8,128)(2,1)S(1)} %get-tuple-element.10), channel_id=1, source_target_pairs={{1,0},{3,2},{5,4},{7,6},{9,8},{11,10},{13,12},{15,14},{17,16},{19,... | collective-permute-start | bytes 98312 | tf_op jit(solution)/shard_map/ppermute | solution.py:49
  112.4 7.7 %copy-start.2 = (bf16[8,8,16,256]{3,1,2,0:T(8,128)(2,1)S(1)}, bf16[8,8,16,256]{3,1,2,0:T(8,128)(2,1)}, u32[]{:S(2)}) copy-start(bf16[8,8,16,256]{3,1,2,0:T(8,128)(2,1)} %copy-done.1) | copy-start | bytes 1572868
  120.4 3.4 %collective-permute-start.19 = (bf16[64,256]{1,0:T(8,128)(2,1)S(1)}, bf16[64,256]{1,0:T(8,128)(2,1)S(1)}, u32[]{:S(2)}, u32[]{:S(2)}) collective-permute-start(bf16[64,256]{1,0:T(8,128)(2,1)S(1)} %get-tuple-element.7), channel_id=1, source_target_pairs={{0,1},{2,3},{4,5},{6,7},{8,9},{10,11},{12,13},{14,15},{16,17},{18,... | collective-permute-start | bytes 98312 | tf_op jit(solution)/shard_map/ppermute | solution.py:46
  122.4 3.1 %collective-permute-start.20 = (bf16[64,256]{1,0:T(8,128)(2,1)S(1)}, bf16[64,256]{1,0:T(8,128)(2,1)S(1)}, u32[]{:S(2)}, u32[]{:S(2)}) collective-permute-start(bf16[64,256]{1,0:T(8,128)(2,1)S(1)} %get-tuple-element.8), channel_id=1, source_target_pairs={{1,0},{3,2},{5,4},{7,6},{9,8},{11,10},{13,12},{15,14},{17,16},{19,... | collective-permute-start | bytes 98312 | tf_op jit(solution)/shard_map/ppermute | solution.py:49
  128.8 7.7 %copy-start.3 = (bf16[8,8,16,256]{3,1,2,0:T(8,128)(2,1)S(1)}, bf16[8,8,16,256]{3,1,2,0:T(8,128)(2,1)}, u32[]{:S(2)}) copy-start(bf16[8,8,16,256]{3,1,2,0:T(8,128)(2,1)} %copy-done.1) | copy-start | bytes 1572868
  136.4 1.0 copy-start.4
  137.4 0.8 copy-start.9
  138.2 14.9 %collective-permute-start.21 = (bf16[64,256]{1,0:T(8,128)(2,1)S(1)}, bf16[64,256]{1,0:T(8,128)(2,1)S(1)}, u32[]{:S(2)}, u32[]{:S(2)}) collective-permute-start(bf16[64,256]{1,0:T(8,128)(2,1)S(1)} %get-tuple-element.5), channel_id=1, source_target_pairs={{0,1},{2,3},{4,5},{6,7},{8,9},{10,11},{12,13},{14,15},{16,17},{18,... | collective-permute-start | bytes 98312 | tf_op jit(solution)/shard_map/ppermute | solution.py:46
  140.3 12.9 %collective-permute-start.22 = (bf16[64,256]{1,0:T(8,128)(2,1)S(1)}, bf16[64,256]{1,0:T(8,128)(2,1)S(1)}, u32[]{:S(2)}, u32[]{:S(2)}) collective-permute-start(bf16[64,256]{1,0:T(8,128)(2,1)S(1)} %get-tuple-element.6), channel_id=1, source_target_pairs={{1,0},{3,2},{5,4},{7,6},{9,8},{11,10},{13,12},{15,14},{17,16},{19,... | collective-permute-start | bytes 98312 | tf_op jit(solution)/shard_map/ppermute | solution.py:49
  145.9 3.1 %copy-start.5 = (f32[32,64,128,1]{2,1,3,0:T(8,128)S(1)}, f32[32,64,128,1]{2,1,3,0:T(8,128)}, u32[]{:S(2)}) copy-start(f32[32,64,128,1]{2,1,3,0:T(8,128)} %copy-done.4) | copy-start | bytes 3145732
  149.0 4.1 %copy-start.10 = (bf16[64,4096]{1,0:T(8,128)(2,1)S(1)}, bf16[64,4096]{1,0:T(8,128)(2,1)}, u32[]{:S(2)}) copy-start(bf16[64,4096]{1,0:T(8,128)(2,1)} %copy-done.9) | copy-start | bytes 1572868
  164.0 4.1 %copy-start.7 = (bf16[16,64,256]{2,1,0:T(8,128)(2,1)S(1)}, bf16[16,64,256]{2,1,0:T(8,128)(2,1)}, u32[]{:S(2)}) copy-start(bf16[16,64,256]{2,1,0:T(8,128)(2,1)} %copy-done.6) | copy-start | bytes 1572868
  164.0 4.1 %copy-start.8 = (f32[64,16,256]{2,1,0:T(8,128)S(1)}, f32[64,16,256]{2,1,0:T(8,128)}, u32[]{:S(2)}) copy-start(f32[64,16,256]{2,1,0:T(8,128)} %reshape.50) | copy-start | bytes 3145732
